TPU v7x, 32 devices: a whole 2x2x4 slice. The times are simulated.
32 devices in a mesh: seq: 8 (over y, x, core), ch: 4 (over z).
Axes of the slice: x: 2, y: 2, z: 4, core: 2. Of those that a mesh axis runs over, the one named last changes fastest.
Arguments:
- projected: float32 [3, 512, 4096], P(None, 'ch', 'seq'), may hold values from -6 to 6
- short_taps: float32 [7, 3, 512], P(None, None, 'ch'), may hold values from -2 to 2
- medium_taps: float32 [128, 512], P(None, 'ch'), may hold values from -0.5 to 0.5
- global_kernel_taps: float32 [512, 4096], P('ch', 'seq')
- residual_coefficient: float32 [512], P('ch'), may hold values from -4 to 4
- mixer_weight: bfloat16 [512, 512], P(None, 'ch'), may hold values from -0.25 to 0.25
Outputs:
- mixed: float32 [512, 4096], P('ch', 'seq')
All inputs are finite; a program needn't handle non-finite values.
Results may differ from a plain program's by a relative error of at most 0.0029.
Values may be sent and summed in bfloat16 or wider, within the bound.
A program may use at most 128 MiB of HBM per device.

v0:
```python
import math

import jax
import jax.numpy as jnp
from jax import lax
from jax.sharding import PartitionSpec as P

HIGHEST = lax.Precision.HIGHEST


def from_behind(shard, axis, by):
    size = lax.axis_size(axis)
    pairs = [(i, i + by) for i in range(size) if 0 <= i + by < size]
    return lax.ppermute(shard, axis, pairs)


def causal_valid(extended, filter_taps, span_out):
    tap_count = filter_taps.shape[0]
    summed = None
    for offset in range(tap_count):
        begin_at = tap_count - 1 - offset
        term = filter_taps[offset][..., None] * extended[..., begin_at : begin_at + span_out]
        summed = term if summed is None else summed + term
    return summed


def square_table(order):
    index = jnp.arange(order, dtype=jnp.int32)
    angle = (index[:, None] * index[None, :] % order).astype(jnp.float32) * (2.0 * math.pi / order)
    return (jnp.cos(angle), jnp.sin(angle))


def make_tables(overall_line_number, adjacent_number):
    first = overall_line_number // 4
    second = 8 * adjacent_number
    padded_len = first * second
    cos_first, sin_first = square_table(first)
    cos_second, sin_second = square_table(second)
    product = (
        jnp.arange(first, dtype=jnp.int32)[:, None] * jnp.arange(second, dtype=jnp.int32)[None, :]
    )
    angle = product.astype(jnp.float32) * (2.0 * math.pi / padded_len)
    return (
        first,
        second,
        padded_len,
        cos_first,
        sin_first,
        cos_second,
        sin_second,
        jnp.cos(angle),
        jnp.sin(angle),
    )


def forward(signal, tables):
    first, second, padded_len, cos_first, sin_first, cos_second, sin_second, twid_cos, twid_sin = (
        tables
    )
    half = first // 2
    blocks = signal.reshape(signal.shape[0], half, second)
    real_one = jnp.einsum("ka,mab->mkb", cos_first[:, :half], blocks, precision=HIGHEST)
    imag_one = -jnp.einsum("ka,mab->mkb", sin_first[:, :half], blocks, precision=HIGHEST)
    real_two = real_one * twid_cos + imag_one * twid_sin
    imag_two = imag_one * twid_cos - real_one * twid_sin
    real_out = jnp.einsum("mkb,bj->mkj", real_two, cos_second, precision=HIGHEST) + jnp.einsum(
        "mkb,bj->mkj", imag_two, sin_second, precision=HIGHEST
    )
    imag_out = jnp.einsum("mkb,bj->mkj", imag_two, cos_second, precision=HIGHEST) - jnp.einsum(
        "mkb,bj->mkj", real_two, sin_second, precision=HIGHEST
    )
    return (real_out, imag_out)


def inverse(spec_real, spec_imag, tables):
    first, second, padded_len, cos_first, sin_first, cos_second, sin_second, twid_cos, twid_sin = (
        tables
    )
    half = first // 2
    real_one = jnp.einsum("mkj,jb->mkb", spec_real, cos_second, precision=HIGHEST) - jnp.einsum(
        "mkj,jb->mkb", spec_imag, sin_second, precision=HIGHEST
    )
    imag_one = jnp.einsum("mkj,jb->mkb", spec_imag, cos_second, precision=HIGHEST) + jnp.einsum(
        "mkj,jb->mkb", spec_real, sin_second, precision=HIGHEST
    )
    real_two = real_one * twid_cos - imag_one * twid_sin
    imag_two = imag_one * twid_cos + real_one * twid_sin
    result = jnp.einsum("ak,mkb->mab", cos_first[:half], real_two, precision=HIGHEST) - jnp.einsum(
        "ak,mkb->mab", sin_first[:half], imag_two, precision=HIGHEST
    )
    return (result / padded_len).reshape(spec_real.shape[0], half * second)


def long_convolve(third_branch_lines, filter_spec, tables):
    val_real, val_imag = forward(third_branch_lines, tables)
    filt_real, filt_imag = filter_spec
    return inverse(
        val_real * filt_real - val_imag * filt_imag,
        val_real * filt_imag + val_imag * filt_real,
        tables,
    )


def shards(
    projected, short_taps, medium_taps, global_kernel_taps, residual_coefficient, mixer_weight
):
    overall_line_number = projected.shape[2]
    chan_local = projected.shape[1]
    adjacent_number = lax.axis_size("seq")
    adjacent_each = chan_local // adjacent_number
    short_span = short_taps.shape[0]
    medium_span = medium_taps.shape[0]
    tables = make_tables(overall_line_number, adjacent_number)
    filter_blocks = global_kernel_taps.reshape(adjacent_number, adjacent_each, overall_line_number)
    short_edge = from_behind(projected[:, :, overall_line_number - (short_span - 1) :], "seq", 1)
    embedded_tokens = causal_valid(
        jnp.concatenate([short_edge, projected], axis=2), short_taps, overall_line_number
    )
    medium_edge = from_behind(
        embedded_tokens[2, :, overall_line_number - (medium_span - 1) :], "seq", 1
    )
    averaged_sequence = causal_valid(
        jnp.concatenate([medium_edge, embedded_tokens[2]], axis=1), medium_taps, overall_line_number
    )
    first_branch_share = embedded_tokens[0]
    second_branch_share = embedded_tokens[1]
    modulating_sequence = second_branch_share * averaged_sequence
    modulating_pieces_array = modulating_sequence.reshape(
        adjacent_number, adjacent_each, overall_line_number
    )
    third_branch_lines = lax.all_to_all(
        modulating_pieces_array, "seq", split_axis=0, concat_axis=2, tiled=True
    )
    filter_piece = lax.all_to_all(filter_blocks, "seq", split_axis=0, concat_axis=2, tiled=True)
    result = long_convolve(third_branch_lines[0], forward(filter_piece[0], tables), tables)
    mixed_response = lax.all_to_all(
        result[None], "seq", split_axis=2, concat_axis=0, tiled=True
    ).reshape(chan_local, overall_line_number)
    multiplied_response = (
        first_branch_share * (mixed_response + residual_coefficient[:, None] * modulating_sequence)
    ).astype(jnp.bfloat16)
    empty = jnp.zeros((mixer_weight.shape[1], overall_line_number), jnp.float32)
    piece = lax.all_gather(multiplied_response, "ch", axis=0, tiled=True)
    weight_rows = lax.slice_in_dim(mixer_weight, 0, piece.shape[0], axis=0)
    return empty + lax.dot_general(
        weight_rows, piece, (((0,), (0,)), ((), ())), preferred_element_type=jnp.float32
    )


def solution(mesh):
    return jax.shard_map(
        shards,
        mesh=mesh,
        in_specs=(
            P(None, "ch", "seq"),
            P(None, None, "ch"),
            P(None, "ch"),
            P("ch", "seq"),
            P("ch"),
            P(None, "ch"),
        ),
        out_specs=P("ch", "seq"),
        check_vma=False,
    )
```

profile of v0, /device:TPU:0, one launch (start us, length us, event | category | flops | bytes accessed | tf_op | source)
XLA Modules:
  0.0 121.7 jit_solution(7036972350850437782)
XLA Ops:
  0.0 5.3 %all-to-all-start.1 = ((f32[8,16,512]{2,1,0:T(8,128)}), f32[8,16,512]{2,1,0:T(8,128)S(1)}, u32[]{:S(2)}, u32[]{:S(2)}) async-start(f32[8,16,512]{2,1,0:T(8,128)} %bitcast.396), calls=%async_computation.1 | async-start | bytes 524288 | tf_op jit(solution)/shard_map/all_to_all | solution.py:134
  5.3 1.0 slice.839
  6.3 2.4 %collective-permute-start = (f32[3,128,6]{2,1,0:T(8,128)S(1)}, f32[3,128,6]{2,1,0:T(8,128)S(1)}, u32[]{:S(2)}, u32[]{:S(2)}) collective-permute-start(f32[3,128,6]{2,1,0:T(8,128)S(1)} %slice.839), channel_id=1, source_target_pairs={{0,4},{4,8},{8,12},{12,16},{16,20},{20,24},{24,28},{1,5},{5,9},{9,... | collective-permute-start | bytes 27656 | tf_op jit(solution)/shard_map/ppermute | solution.py:14
  8.8 1.0 slice_bitcast_fusion.129
  9.8 1.0 slice_bitcast_fusion.131
  10.8 1.2 %slice_bitcast_fusion.132 = (f32[128]{0:T(128)S(1)}, f32[128]{0:T(128)S(1)}, f32[128]{0:T(128)S(1)}, f32[128]{0:T(128)S(1)}, f32[128]{0:T(128)S(1)}, /*index=5*/...) fusion(f32[128,128]{1,0:T(8,128)} %param.8), kind=kLoop, calls=%fused_computation.887 | loop fusion | bytes 19456 | tf_op jit(solution)/shard_map/mul | solution.py:22
  12.0 1.0 slice_bitcast_fusion.133
  13.0 1.0 slice_bitcast_fusion.134
  14.0 1.1 slice_bitcast_fusion.135
  15.2 1.0 slice_bitcast_fusion.130
  16.7 1.0 fusion.522
  17.9 4.9 %fusion.6 = f32[3,128,512]{2,1,0:T(8,128)S(1)} fusion(f32[3,128,512]{2,1,0:T(8,128)} %param.6, f32[3,128,6]{2,1,0:T(8,128)S(1)} %collective-permute-done, f32[3,128]{1,0:T(4,128)S(1)} %get-tuple-element.142, f32[3,128]{1,0:T(4,128)S(1)} %get-tuple-element.143, f32[3,128]{1,0:T(4,128)S(1)} %get-tuple-element.144, f32[3,128]{1,0:T(4,128)S(1)} %get-tuple-element.145, ...), kind=kLoop, calls=%fused_computation.278 | loop fusion | flops 3735552 | bytes 1592832 | tf_op jit(solution)/shard_map/add | solution.py:23
  22.9 3.5 %collective-permute-start.1 = (f32[128,127]{1,0:T(8,128)S(1)}, f32[128,127]{1,0:T(8,128)S(1)}, u32[]{:S(2)}, u32[]{:S(2)}) collective-permute-start(f32[128,127]{1,0:T(8,128)S(1)} %slice_bitcast_fusion.7), channel_id=1, source_target_pairs={{0,4},{4,8},{8,12},{12,16},{16,20},{20,24},{24,28},{1,5},{5,9},{9,... | collective-permute-start | bytes 195080 | tf_op jit(solution)/shard_map/ppermute | solution.py:14
  26.5 0.9 collective-permute-done.1
  27.3 15.0 %fusion.37 = f32[128,512]{1,0:T(8,128)} fusion(f32[128,512]{1,0:T(8,128)S(1)} %slice_bitcast_fusion, f32[128,127]{1,0:T(8,128)S(1)} %collective-permute-done.1, f32[3,128,512]{2,1,0:T(8,128)S(1)} %fusion.6, f32[128]{0:T(128)S(1)} %get-tuple-element.133, f32[128]{0:T(128)S(1)} %get-tuple-element.134, f32[128]{0:T(128)S(1)} %get-tuple-element.8, ...), kind=kLoop, calls=%fused_computation.316 | loop fusion | flops 25100288 | bytes 916992 | tf_op jit(solution)/shard_map/mul | solution.py:127
  42.3 5.0 %all-to-all-start = ((f32[8,16,512]{2,1,0:T(8,128)}), f32[8,16,512]{2,1,0:T(8,128)S(1)}, u32[]{:S(2)}, u32[]{:S(2)}) async-start(f32[8,16,512]{2,1,0:T(8,128)} %bitcast.132), calls=%async_computation | async-start | bytes 524288 | tf_op jit(solution)/shard_map/all_to_all | solution.py:131
  50.6 0.8 convolution_subtract_fusion.2
  51.4 1.6 %convolution_add_fusion.1 = f32[16,128,64]{1,2,0:T(8,128)} fusion(f32[16,128,64]{1,2,0:T(8,128)S(1)} %fusion.24, f32[128,16,64]{0,2,1:T(8,128)S(1)} %bitcast.388, f32[128,16,64]{0,2,1:T(8,128)S(1)} %bitcast.384, f32[128,64]{0,1:T(8,128)S(1)} %get-tuple-element.148, f32[128,64]{0,1:T(8,128)S(1)} %get-tuple-element.149), kind=kOutput, calls=%fused_computation.267 | convolution fusion | flops 101376000 | bytes 2162688 | tf_op jit(solution)/shard_map/mkb,bj->mkj/dot_general | solution.py:66
  53.0 1.3 %all-to-all-done = f32[8,16,512]{2,1,0:T(8,128)S(1)} async-done(((f32[8,16,512]{2,1,0:T(8,128)}), f32[8,16,512]{2,1,0:T(8,128)S(1)}, u32[]{:S(2)}, u32[]{:S(2)}) %all-to-all-start) | async-done | bytes 262176 | tf_op jit(solution)/shard_map/all_to_all | solution.py:131
  54.6 1.0 fusion
  55.6 1.0 convolution_bitcast_fusion
  58.9 0.9 multiply_subtract_fusion
  61.3 1.0 convolution_subtract_fusion.1
  64.2 1.9 %copy.50 = f32[16,64,64]{0,2,1:T(8,128)S(1)} copy(f32[16,64,64]{1,2,0:T(8,128)S(1)} %fusion.2) | data formatting | bytes 524288 | tf_op jit(solution)/shard_map/broadcast_in_dim;reshape | solution.py:137
  66.6 19.3 %reduce = f32[4096,16]{1,0:T(8,128)} reduce(f32[4096,1,16]{2,1,0:T(1,128)S(1)} %bitcast.389, f32[]{:T(128)} %broadcast.87), dimensions={1}, to_apply=%bitcast.366.reduce_sub_computation | reduce | bytes 524292
  86.0 2.4 %reshape.186 = f32[8,1,8192]{2,1,0:T(1,128)S(1)} reshape(f32[4096,16]{1,0:T(8,128)} %reduce) | data formatting | bytes 524288
  88.4 9.7 %all_to_all.45 = f32[8,1,8192]{2,1,0:T(1,128)S(1)} all-to-all(f32[8,1,8192]{2,1,0:T(1,128)S(1)} %reshape.186), channel_id=1, replica_groups=mesh['seq'=8,'ch'=4] {'seq'}, dimensions={0} | all-to-all | bytes 524288 | tf_op jit(solution)/shard_map/all_to_all | solution.py:136
  98.0 1.2 %reduce.1 = f32[8,8192]{1,0:T(8,128)S(1)} reduce(f32[8,1,8192]{2,1,0:T(1,128)S(1)} %all_to_all.45, f32[]{:T(128)} %broadcast.87), dimensions={1}, to_apply=%all_to_all.39.reduce_sub_computation | reduce | bytes 524292 | tf_op jit(solution)/shard_map/all_to_all | solution.py:136
  99.3 3.9 %reshape.187 = f32[4096,1,16]{2,1,0:T(1,128)S(1)} reshape(f32[8,8192]{1,0:T(8,128)S(1)} %reduce.1) | data formatting | bytes 524288
  104.0 1.1 fusion.415
  105.1 15.4 %all_gather.3 = bf16[512,512]{1,0:T(8,128)(2,1)S(1)} all-gather(bf16[128,512]{1,0:T(8,128)(2,1)S(1)} %fusion.415), channel_id=1, replica_groups=mesh['seq'=8,'ch'=4] {'ch'}, dimensions={0}, use_global_device_ids=true | all-gather | bytes 655360 | tf_op jit(solution)/shard_map/all_gather | solution.py:143
  120.8 0.8 copy.43
  (38 shorter events, 11.6 us)
Async XLA Ops:
  0.0 120.5 %copy-start = (bf16[512,128]{1,0:T(8,128)(2,1)S(1)}, bf16[512,128]{1,0:T(8,128)(2,1)}, u32[]{:S(2)}) copy-start(bf16[512,128]{1,0:T(8,128)(2,1)} %param.11) | copy-start | bytes 393220
  0.0 42.3 %all-to-all-start.1 = ((f32[8,16,512]{2,1,0:T(8,128)}), f32[8,16,512]{2,1,0:T(8,128)S(1)}, u32[]{:S(2)}, u32[]{:S(2)}) async-start(f32[8,16,512]{2,1,0:T(8,128)} %bitcast.396), calls=%async_computation.1 | async-start | bytes 524288 | tf_op jit(solution)/shard_map/all_to_all | solution.py:134
  6.3 11.5 %collective-permute-start = (f32[3,128,6]{2,1,0:T(8,128)S(1)}, f32[3,128,6]{2,1,0:T(8,128)S(1)}, u32[]{:S(2)}, u32[]{:S(2)}) collective-permute-start(f32[3,128,6]{2,1,0:T(8,128)S(1)} %slice.839), channel_id=1, source_target_pairs={{0,4},{4,8},{8,12},{12,16},{16,20},{20,24},{24,28},{1,5},{5,9},{9,... | collective-permute-start | bytes 27656 | tf_op jit(solution)/shard_map/ppermute | solution.py:14
  22.9 4.4 %collective-permute-start.1 = (f32[128,127]{1,0:T(8,128)S(1)}, f32[128,127]{1,0:T(8,128)S(1)}, u32[]{:S(2)}, u32[]{:S(2)}) collective-permute-start(f32[128,127]{1,0:T(8,128)S(1)} %slice_bitcast_fusion.7), channel_id=1, source_target_pairs={{0,4},{4,8},{8,12},{12,16},{16,20},{20,24},{24,28},{1,5},{5,9},{9,... | collective-permute-start | bytes 195080 | tf_op jit(solution)/shard_map/ppermute | solution.py:14
  42.3 11.9 %all-to-all-start = ((f32[8,16,512]{2,1,0:T(8,128)}), f32[8,16,512]{2,1,0:T(8,128)S(1)}, u32[]{:S(2)}, u32[]{:S(2)}) async-start(f32[8,16,512]{2,1,0:T(8,128)} %bitcast.132), calls=%async_computation | async-start | bytes 524288 | tf_op jit(solution)/shard_map/all_to_all | solution.py:131
  57.4 1.6 %copy-start.1 = (f32[16,128,64]{1,2,0:T(8,128)S(1)}, f32[16,128,64]{1,2,0:T(8,128)}, u32[]{:S(2)}) copy-start(f32[16,128,64]{1,2,0:T(8,128)} %convolution_add_fusion.1) | copy-start | bytes 1572868
  99.3 4.8 %copy-start.2 = (f32[128]{0:T(128)S(1)}, f32[128]{0:T(128)}, u32[]{:S(2)}) copy-start(f32[128]{0:T(128)} %param.10) | copy-start | bytes 1540
where the time goes:
time: 123 us; the launch traced here: 122 us
  other arithmetic  42.2 us (34%)
  blocking collectives  25.1 us (20%)
  local copies, waits for them, and re-layouts  20.6 us (17%)
  starting transfers between devices  16.3 us (13%)
  matrix products  15 us (12%)
  waiting for transfers between devices  2.12 us (2%)
    unnamed x1, other arithmetic  19.3 us
    all_gather x1, blocking collectives, shards(): piece = lax.all_gather(multiplied_response, 'ch', axis=0, tiled=True)  15.4 us
    mul x1, other arithmetic, shards(): modulating_sequence = second_branch_share * averaged_sequence  15 us
    all_to_all x1, blocking collectives, shards(): lax.all_to_all(result[None], 'seq', split_axis=2, concat_axis=0, tiled=True)  9.67 us
    mul x7, local copies, waits for them, and re-layouts, causal_valid(): filter_taps[offset][..., None] * extended[..., begin_at:begin_at + span_out]  7.39 us
    unnamed x13, local copies, waits for them, and re-layouts  6.89 us
    ppermute x2, starting transfers between devices, from_behind(): return lax.ppermute(shard, axis, pairs)  5.95 us
    all_to_all x1, starting transfers between devices, shards(): lax.all_to_all(filter_blocks, 'seq', split_axis=0, concat_axis=2, tiled=T...  5.3 us
  transfers between devices with their start and end apart: 4, of which 2 were waited for; matrix products, arithmetic and copies ran while one was open for 29% of the time, Pallas kernels for 0%

commit v1 on v0

--- a/solution.py
+++ b/solution.py
@@ -1,8 +1,12 @@
+import functools
 import math
 
 import jax
 import jax.numpy as jnp
+import numpy as np
 from jax import lax
+from jax.experimental import pallas as pl
+from jax.experimental.pallas import tpu as pltpu
 from jax.sharding import PartitionSpec as P
 
 HIGHEST = lax.Precision.HIGHEST
@@ -147,9 +151,410 @@
     )
 
 
+LANES = 128
+HALO = 136
+MESH = pl.DeviceIdType.MESH
+
+
+def split_np(table):
+    high = table.astype(np.float32).astype(jnp.bfloat16)
+    low = (table - high.astype(np.float64)).astype(np.float32).astype(jnp.bfloat16)
+    return high, low
+
+
+def spectral_tables(rows):
+    span = rows * LANES
+    index = np.arange(rows, dtype=np.float64)
+    lane = np.arange(LANES, dtype=np.float64)
+    first = 2 * np.pi * np.outer(index + 0.25, index) / rows
+    twiddle = 2 * np.pi * np.outer(index + 0.25, lane) / span
+    second = 2 * np.pi * np.outer(lane, lane) / LANES
+    into = np.concatenate([np.cos(first), -np.sin(first)], axis=0)
+    high, low = split_np(into)
+    into = np.concatenate([high, high, low], axis=1)
+    back = np.concatenate([np.cos(first).T, -np.sin(first).T], axis=1) / span
+    high, low = split_np(back)
+    back = np.concatenate([high, high, low], axis=1)
+    cos, sin = np.cos(second), np.sin(second)
+    ahead = np.block([[cos, -sin], [sin, cos]])
+    ahead = np.stack(split_np(ahead))
+    behind = np.block([[cos, sin], [-sin, cos]])
+    behind = np.stack(split_np(behind))
+    turn = np.stack([np.cos(twiddle), np.sin(twiddle)]).astype(np.float32)
+    return into, back, ahead, behind, turn
+
+
+def split(value):
+    high = value.astype(jnp.bfloat16)
+    low = (value - high.astype(jnp.float32)).astype(jnp.bfloat16)
+    return high, low
+
+
+def dot(left, right):
+    return jnp.dot(left, right, preferred_element_type=jnp.float32)
+
+
+def dot3(value, table_ref):
+    high, low = split(value)
+    return dot(high, table_ref[0]) + dot(low, table_ref[0]) + dot(high, table_ref[1])
+
+
+def to_spectrum(src, spec, each, rows, into_ref, ahead_ref, turn_ref):
+    cos, sin = turn_ref[0], turn_ref[1]
+    group = 4
+    for begin in range(0, each, group):
+        lines = [src[pl.ds(begin + i, rows, stride=each), :] for i in range(group)]
+        high, low = split(jnp.concatenate(lines, axis=1))
+        once = dot(into_ref[...], jnp.concatenate([high, low, high], axis=0))
+        turned = []
+        for i in range(group):
+            real = once[:rows, i * LANES : (i + 1) * LANES]
+            imag = once[rows:, i * LANES : (i + 1) * LANES]
+            turned.append(
+                jnp.concatenate([real * cos + imag * sin, imag * cos - real * sin], axis=1)
+            )
+        twice = dot3(jnp.concatenate(turned, axis=0), ahead_ref)
+        spec[begin * rows : (begin + group) * rows, :] = twice
+
+
+def from_spectrum(val, filt, dst, each, rows, back_ref, behind_ref, turn_ref):
+    cos, sin = turn_ref[0], turn_ref[1]
+    group = 4
+    for begin in range(0, each, group):
+        part = slice(begin * rows, (begin + group) * rows)
+        val_real, val_imag = val[part, :LANES], val[part, LANES:]
+        filt_real, filt_imag = filt[part, :LANES], filt[part, LANES:]
+        product = jnp.concatenate(
+            [
+                val_real * filt_real - val_imag * filt_imag,
+                val_real * filt_imag + val_imag * filt_real,
+            ],
+            axis=1,
+        )
+        once = dot3(product, behind_ref)
+        turned = []
+        for i in range(group):
+            real = once[i * rows : (i + 1) * rows, :LANES]
+            imag = once[i * rows : (i + 1) * rows, LANES:]
+            turned.append(
+                jnp.concatenate([real * cos - imag * sin, imag * cos + real * sin], axis=0)
+            )
+        high, low = split(jnp.concatenate(turned, axis=1))
+        lines = dot(back_ref[...], jnp.concatenate([high, low, high], axis=0))
+        for i in range(group):
+            dst[pl.ds(begin + i, rows, stride=each), :] = lines[:, i * LANES : (i + 1) * LANES]
+
+
+def kernel(
+    seq_size,
+    ch_size,
+    proj_ref,
+    short_ref,
+    medium_ref,
+    taps_ref,
+    resid_ref,
+    mix_ref,
+    into_ref,
+    back_ref,
+    ahead_ref,
+    behind_ref,
+    turn_ref,
+    out_ref,
+    lines_t,
+    feat_v,
+    taps_out,
+    taps_in,
+    carrier,
+    carrier_in,
+    gate,
+    answer,
+    answer_in,
+    spec_filt,
+    spec_val,
+    gated,
+    halo_send,
+    halo_recv,
+    taps_send,
+    taps_recv,
+    carrier_send,
+    carrier_recv,
+    answer_send,
+    answer_recv,
+    gated_send,
+    gated_recv,
+):
+    me = lax.axis_index("seq")
+    group = lax.axis_index("ch")
+    chan, span = proj_ref.shape[1], proj_ref.shape[2]
+    short_span = short_ref.shape[0]
+    medium_span = medium_ref.shape[0]
+    each = chan // seq_size
+    blocks = span // LANES
+    rows = seq_size * blocks
+    slab = blocks * each
+
+    barrier = pltpu.get_barrier_semaphore()
+    for step in range(1, seq_size):
+        pl.semaphore_signal(
+            barrier, 1, device_id={"seq": lax.rem(me + step, seq_size)}, device_id_type=MESH
+        )
+    for step in range(1, ch_size):
+        pl.semaphore_signal(
+            barrier, 1, device_id={"ch": lax.rem(group + step, ch_size)}, device_id_type=MESH
+        )
+
+    def transpose_in(stream):
+        for k in range(blocks):
+            lines_t[stream, HALO + k * LANES : HALO + (k + 1) * LANES, :] = proj_ref[
+                stream, :, k * LANES : (k + 1) * LANES
+            ].T
+
+    def scatter_rows(dst, k, block):
+        for s in range(seq_size):
+            dst[s * slab + k * each : s * slab + (k + 1) * each, :] = block[
+                s * each : (s + 1) * each, :
+            ]
+
+    transpose_in(2)
+    for k in range(blocks):
+        scatter_rows(taps_out, k, taps_ref[:, k * LANES : (k + 1) * LANES])
+    transpose_in(1)
+    transpose_in(0)
+    pl.semaphore_wait(barrier, seq_size - 1 + ch_size - 1)
+
+    def halo_copies():
+        after = lax.rem(me + 1, seq_size)
+        return [
+            pltpu.make_async_remote_copy(
+                src_ref=lines_t.at[2, span : span + HALO, :],
+                dst_ref=lines_t.at[2, 0:HALO, :],
+                send_sem=halo_send.at[0],
+                recv_sem=halo_recv.at[0],
+                device_id={"seq": after},
+                device_id_type=MESH,
+            ),
+            pltpu.make_async_remote_copy(
+                src_ref=lines_t.at[0:2, span + HALO - 8 : span + HALO, :],
+                dst_ref=lines_t.at[0:2, HALO - 8 : HALO, :],
+                send_sem=halo_send.at[1],
+                recv_sem=halo_recv.at[1],
+                device_id={"seq": after},
+                device_id_type=MESH,
+            ),
+        ]
+
+    @pl.when(me < seq_size - 1)
+    def _():
+        for copy in halo_copies():
+            copy.start()
+
+    def exchange(src, dst, send, recv):
+        copies = []
+        for step in range(1, seq_size):
+            peer = lax.rem(me + step, seq_size)
+            copies.append(
+                pltpu.make_async_remote_copy(
+                    src_ref=src.at[pl.ds(pl.multiple_of(peer * slab, 8), slab), :],
+                    dst_ref=dst.at[pl.ds(pl.multiple_of(me * slab, 8), slab), :],
+                    send_sem=send.at[step],
+                    recv_sem=recv.at[step],
+                    device_id={"seq": peer},
+                    device_id_type=MESH,
+                )
+            )
+        for copy in copies:
+            copy.start()
+        own = pl.ds(pl.multiple_of(me * slab, 8), slab)
+        dst[own, :] = src[own, :]
+        return copies
+
+    taps_copies = exchange(taps_out, taps_in, taps_send, taps_recv)
+
+    @pl.when(me == 0)
+    def _():
+        lines_t[2, 0:HALO, :] = jnp.zeros((HALO, chan), jnp.float32)
+        lines_t[0:2, HALO - 8 : HALO, :] = jnp.zeros((2, 8, chan), jnp.float32)
+
+    @pl.when(me > 0)
+    def _():
+        for copy in halo_copies():
+            copy.wait_recv()
+
+    def short(stream, begin, count):
+        total = None
+        for j in range(short_span):
+            term = (
+                short_ref[j, stream : stream + 1, :]
+                * lines_t[stream, begin - j : begin - j + count, :]
+            )
+            total = term if total is None else total + term
+        return total
+
+    for begin in range(0, LANES + span, LANES):
+        feat_v[begin : begin + LANES, :] = short(2, HALO - LANES + begin, LANES)
+
+    tile = 8
+
+    for k in range(blocks):
+        base = (k + 1) * LANES
+
+        def taps_body(m, total):
+            for r in range(tile):
+                j = m * tile + r
+                start = base - r - m * tile
+                total = total + medium_ref[pl.ds(j, 1), :] * feat_v[pl.ds(start, LANES), :]
+            return total
+
+        smooth = lax.fori_loop(
+            0, medium_span // tile, taps_body, jnp.zeros((LANES, chan), jnp.float32)
+        )
+        block = short(1, HALO + k * LANES, LANES) * smooth
+        scatter_rows(carrier, k, block.T)
+
+    carrier_copies = exchange(carrier, carrier_in, carrier_send, carrier_recv)
+
+    for copy in taps_copies:
+        copy.wait_recv()
+    to_spectrum(taps_in, spec_filt, each, rows, into_ref, ahead_ref, turn_ref)
+    for k in range(blocks):
+        scatter_rows(gate, k, short(0, HALO + k * LANES, LANES).T)
+    resid = jnp.broadcast_to(resid_ref[...], (LANES, chan)).T
+
+    for copy in carrier_copies:
+        copy.wait_recv()
+    to_spectrum(carrier_in, spec_val, each, rows, into_ref, ahead_ref, turn_ref)
+    from_spectrum(spec_val, spec_filt, answer, each, rows, back_ref, behind_ref, turn_ref)
+    answer_copies = exchange(answer, answer_in, answer_send, answer_recv)
+    for copy in answer_copies:
+        copy.wait_recv()
+
+    for s in range(seq_size):
+        weight = resid[s * each : (s + 1) * each, :]
+        for k in range(blocks):
+            part = slice(s * slab + k * each, s * slab + (k + 1) * each)
+            value = gate[part, :] * (answer_in[part, :] + weight * carrier[part, :])
+            gated[group, s * each : (s + 1) * each, k * LANES : (k + 1) * LANES] = value.astype(
+                jnp.bfloat16
+            )
+
+    gated_copies = []
+    for step in range(1, ch_size):
+        copy = pltpu.make_async_remote_copy(
+            src_ref=gated.at[group],
+            dst_ref=gated.at[group],
+            send_sem=gated_send.at[step],
+            recv_sem=gated_recv.at[step],
+            device_id={"ch": lax.rem(group + step, ch_size)},
+            device_id_type=MESH,
+        )
+        copy.start()
+        gated_copies.append(copy)
+
+    def mixed(owner):
+        weight = mix_ref[pl.ds(pl.multiple_of(owner * chan, LANES), chan), :]
+        return lax.dot_general(
+            weight, gated[owner], (((0,), (0,)), ((), ())), preferred_element_type=jnp.float32
+        )
+
+    total = mixed(group)
+    for step in range(1, ch_size):
+        gated_copies[step - 1].wait_recv()
+        total = total + mixed(lax.rem(group - step + ch_size, ch_size))
+    out_ref[...] = total
+
+    @pl.when(me < seq_size - 1)
+    def _():
+        for copy in halo_copies():
+            copy.wait_send()
+
+    for copy in taps_copies + carrier_copies + answer_copies + gated_copies:
+        copy.wait_send()
+
+
+def fused(
+    projected, short_taps, medium_taps, global_kernel_taps, residual_coefficient, mixer_weight
+):
+    seq_size, ch_size = lax.axis_size("seq"), lax.axis_size("ch")
+    chan, span = projected.shape[1], projected.shape[2]
+    each = chan // seq_size
+    rows = seq_size * span // LANES
+    tables = [jnp.asarray(table) for table in spectral_tables(rows)]
+    vmem = pl.BlockSpec(memory_space=pltpu.VMEM)
+    plane = pltpu.VMEM((chan * span // LANES, LANES), jnp.float32)
+    spectrum = pltpu.VMEM((each * rows, 2 * LANES), jnp.float32)
+    dma = pltpu.SemaphoreType.DMA
+    return pl.pallas_call(
+        functools.partial(kernel, seq_size, ch_size),
+        out_shape=jax.ShapeDtypeStruct((mixer_weight.shape[1], span), jnp.float32),
+        in_specs=[vmem] * 11,
+        out_specs=vmem,
+        scratch_shapes=[
+            pltpu.VMEM((3, HALO + span, chan), jnp.float32),
+            pltpu.VMEM((LANES + span, chan), jnp.float32),
+            plane,
+            plane,
+            plane,
+            plane,
+            plane,
+            plane,
+            plane,
+            spectrum,
+            spectrum,
+            pltpu.VMEM((ch_size, chan, span), jnp.bfloat16),
+            dma((2,)),
+            dma((2,)),
+            dma((seq_size,)),
+            dma((seq_size,)),
+            dma((seq_size,)),
+            dma((seq_size,)),
+            dma((seq_size,)),
+            dma((seq_size,)),
+            dma((ch_size,)),
+            dma((ch_size,)),
+        ],
+        compiler_params=pltpu.CompilerParams(
+            collective_id=0, has_side_effects=True, vmem_limit_bytes=40 * 2**20
+        ),
+        name="hyena",
+    )(
+        projected,
+        short_taps,
+        medium_taps,
+        global_kernel_taps,
+        residual_coefficient.reshape(1, chan),
+        mixer_weight,
+        *tables,
+    )
+
+
+def block(
+    projected, short_taps, medium_taps, global_kernel_taps, residual_coefficient, mixer_weight
+):
+    operands = (
+        projected,
+        short_taps,
+        medium_taps,
+        global_kernel_taps,
+        residual_coefficient,
+        mixer_weight,
+    )
+    chan, span = projected.shape[1], projected.shape[2]
+    each = chan // lax.axis_size("seq")
+    fits = (
+        chan == LANES
+        and span % LANES == 0
+        and span >= HALO
+        and each % 16 == 0
+        and medium_taps.shape[0] == LANES
+        and short_taps.shape[0] <= 8
+        and chan * span * 4 <= 2**20
+    )
+    return fused(*operands) if fits else shards(*operands)
+
+
 def solution(mesh):
     return jax.shard_map(
-        shards,
+        block,
         mesh=mesh,
         in_specs=(
             P(None, "ch", "seq"),

time: 123 us -> 43.3 us (0.35)
  other arithmetic: 42.2 us -> 0 us
  Pallas kernels: 0 us -> 34.2 us
  blocking collectives: 25.1 us -> 0 us
  starting transfers between devices: 16.3 us -> 0 us
  matrix products: 15 us -> 0 us
  local copies, waits for them, and re-layouts: 20.6 us -> 8.64 us
  waiting for transfers between devices: 2.12 us -> 0 us
    pallas_call x0 -> x1, Pallas kernels: none -> 34.2 us  [fused(): pl.pallas_call(functools.partial(kernel, seq_size, ch_size), out_shape=ja...]
    unnamed x1 -> x0, other arithmetic: 19.3 us -> none
    all_gather x1 -> x0, blocking collectives: 15.4 us -> none  [shards(): piece = lax.all_gather(multiplied_response, 'ch', axis=0, tiled=True)]
    mul x1 -> x0, other arithmetic: 15 us -> none  [shards(): modulating_sequence = second_branch_share * averaged_sequence]
    dot_general x17 -> x0, matrix products: 13.9 us -> none  [the longest x2 2.39 us: forward(): jnp.einsum('mkb,bj->mkj', imag_two, sin_second, precision=HIGHEST)]
    all_to_all x2 -> x0, starting transfers between devices: 10.3 us -> none  [the longest x1 5.3 us: shards(): lax.all_to_all(filter_blocks, 'seq', split_axis=0, concat_axis=2, tiled=T...]
    all_to_all x1 -> x0, blocking collectives: 9.67 us -> none  [shards(): lax.all_to_all(result[None], 'seq', split_axis=2, concat_axis=0, tiled=True)]
    mul x7 -> x0, local copies, waits for them, and re-layouts: 7.39 us -> none  [causal_valid(): filter_taps[offset][..., None] * extended[..., begin_at:begin_at + span_out]]
  transfers between devices with their start and end apart: 4 -> 0, of which waited for: 2 -> 0; matrix products, arithmetic and copies ran while one was open for 29% -> 0% of each run, Pallas kernels for 0% -> 0%
where the time goes in v1:
time: 43.3 us; the launch traced here: 42.8 us
  Pallas kernels  34.2 us (79%)
  local copies, waits for them, and re-layouts  8.64 us (20%)
    pallas_call x1, Pallas kernels, fused(): pl.pallas_call(functools.partial(kernel, seq_size, ch_size), out_shape=ja...  34.2 us
    unnamed x22, local copies, waits for them, and re-layouts  8.64 us

profile of v1, /device:TPU:0, one launch (start us, length us, event | category | flops | bytes accessed | tf_op | source)
XLA Modules:
  0.0 42.8 jit_solution(8064400231768602903)
XLA Ops:
  0.0 0.0 copy-start.6
  0.0 0.0 copy-start.9
  0.0 0.7 %copy.12.short_ref = f32[7,3,128]{2,1,0:T(4,128)S(1)} copy(f32[7,3,128]{2,0,1:T(8,128)} %param.12) | data formatting | bytes 21504 | tf_op args[1]
  0.7 0.1 copy-done.6
  0.8 0.0 copy-done.9
  0.8 0.0 copy-start
  0.8 1.1 %copy-done = f32[3,128,512]{2,1,0:T(8,128)S(1)} copy-done((f32[3,128,512]{2,1,0:T(8,128)S(1)}, f32[3,128,512]{2,1,0:T(8,128)}, u32[]{:S(2)}) %copy-start) | copy-done | bytes 786456
  1.9 0.0 copy-start.1
  1.9 0.9 %copy-done.1 = f32[128,512]{1,0:T(8,128)S(1)} copy-done((f32[128,512]{1,0:T(8,128)S(1)}, f32[128,512]{1,0:T(8,128)}, u32[]{:S(2)}) %copy-start.1) | copy-done | bytes 262168
  2.9 0.0 copy-start.2
  2.9 0.9 %copy-done.2 = bf16[2,256,256]{2,1,0:T(8,128)(2,1)S(1)} copy-done((bf16[2,256,256]{2,1,0:T(8,128)(2,1)S(1)}, bf16[2,256,256]{2,1,0:T(8,128)(2,1)}, u32[]{:S(2)}) %copy-start.2) | copy-done | bytes 262168
  3.8 0.0 copy-start.3
  3.8 0.9 %copy-done.3 = bf16[2,256,256]{2,1,0:T(8,128)(2,1)S(1)} copy-done((bf16[2,256,256]{2,1,0:T(8,128)(2,1)S(1)}, bf16[2,256,256]{2,1,0:T(8,128)(2,1)}, u32[]{:S(2)}) %copy-start.3) | copy-done | bytes 262168
  4.8 0.0 copy-start.4
  4.8 0.9 %copy-done.4 = bf16[512,128]{1,0:T(8,128)(2,1)S(1)} copy-done((bf16[512,128]{1,0:T(8,128)(2,1)S(1)}, bf16[512,128]{1,0:T(8,128)(2,1)}, u32[]{:S(2)}) %copy-start.4) | copy-done | bytes 131096
  5.7 0.0 copy-start.5
  5.7 0.8 %copy-done.5 = f32[128,128]{1,0:T(8,128)S(1)} copy-done((f32[128,128]{1,0:T(8,128)S(1)}, f32[128,128]{1,0:T(8,128)}, u32[]{:S(2)}) %copy-start.5) | copy-done | bytes 65560
  6.5 0.0 copy-start.7
  6.5 0.7 %copy-done.7 = bf16[32,192]{1,0:T(8,128)(2,1)S(1)} copy-done((bf16[32,192]{1,0:T(8,128)(2,1)S(1)}, bf16[32,192]{1,0:T(8,128)(2,1)}, u32[]{:S(2)}) %copy-start.7) | copy-done | bytes 12312
  7.2 0.0 copy-start.8
  7.2 0.7 %copy-done.8 = bf16[64,96]{1,0:T(8,128)(2,1)S(1)} copy-done((bf16[64,96]{1,0:T(8,128)(2,1)S(1)}, bf16[64,96]{1,0:T(8,128)(2,1)}, u32[]{:S(2)}) %copy-start.8) | copy-done | bytes 12312
  7.9 34.2 %hyena.1 = f32[128,512]{1,0:T(8,128)S(1)} custom-call(f32[3,128,512]{2,1,0:T(8,128)S(1)} %copy-done, f32[7,3,128]{2,1,0:T(4,128)S(1)} %copy.12.short_ref, f32[128,128]{1,0:T(8,128)S(1)} %copy-done.5, f32[128,512]{1,0:T(8,128)S(1)} %copy-done.1, f32[1,128]{1,0:T(1,128)S(1)} %bitcast.1, bf16[512,128]{1,0:T(8,128)(2,1)S(1)} %copy-done.4, ...), custom_call_target="tpu_custom_call" | custom-call | tf_op jit(solution)/shard_map/hyena/pallas_call | solution.py:486
  42.1 0.7 %copy.14 = f32[128,512]{1,0:T(8,128)} copy(f32[128,512]{1,0:T(8,128)S(1)} %hyena.1) | data formatting | bytes 524288
Async XLA Ops:
  0.0 0.8 %copy-start.6 = (f32[2,32,128]{2,1,0:T(8,128)S(1)}, f32[2,32,128]{2,1,0:T(8,128)}, u32[]{:S(2)}) copy-start(f32[2,32,128]{2,1,0:T(8,128)} %constant.14.clone.turn_ref) | copy-start | bytes 98308
  0.0 0.8 %copy-start.9 = (f32[128]{0:T(128)S(1)}, f32[128]{0:T(128)}, u32[]{:S(2)}) copy-start(f32[128]{0:T(128)} %param.15) | copy-start | bytes 1540
  0.8 1.1 %copy-start = (f32[3,128,512]{2,1,0:T(8,128)S(1)}, f32[3,128,512]{2,1,0:T(8,128)}, u32[]{:S(2)}) copy-start(f32[3,128,512]{2,1,0:T(8,128)} %proj_ref.1) | copy-start | bytes 2359300
  1.9 0.9 %copy-start.1 = (f32[128,512]{1,0:T(8,128)S(1)}, f32[128,512]{1,0:T(8,128)}, u32[]{:S(2)}) copy-start(f32[128,512]{1,0:T(8,128)} %taps_ref.1) | copy-start | bytes 786436
  2.9 0.9 %copy-start.2 = (bf16[2,256,256]{2,1,0:T(8,128)(2,1)S(1)}, bf16[2,256,256]{2,1,0:T(8,128)(2,1)}, u32[]{:S(2)}) copy-start(bf16[2,256,256]{2,1,0:T(8,128)(2,1)} %constant.13.clone.behind_ref) | copy-start | bytes 786436
  3.8 0.9 %copy-start.3 = (bf16[2,256,256]{2,1,0:T(8,128)(2,1)S(1)}, bf16[2,256,256]{2,1,0:T(8,128)(2,1)}, u32[]{:S(2)}) copy-start(bf16[2,256,256]{2,1,0:T(8,128)(2,1)} %constant.12.clone.ahead_ref) | copy-start | bytes 786436
  4.8 0.9 %copy-start.4 = (bf16[512,128]{1,0:T(8,128)(2,1)S(1)}, bf16[512,128]{1,0:T(8,128)(2,1)}, u32[]{:S(2)}) copy-start(bf16[512,128]{1,0:T(8,128)(2,1)} %mix_ref.1) | copy-start | bytes 393220
  5.7 0.8 %copy-start.5 = (f32[128,128]{1,0:T(8,128)S(1)}, f32[128,128]{1,0:T(8,128)}, u32[]{:S(2)}) copy-start(f32[128,128]{1,0:T(8,128)} %medium_ref.1) | copy-start | bytes 196612
  6.5 0.7 %copy-start.7 = (bf16[32,192]{1,0:T(8,128)(2,1)S(1)}, bf16[32,192]{1,0:T(8,128)(2,1)}, u32[]{:S(2)}) copy-start(bf16[32,192]{1,0:T(8,128)(2,1)} %constant.11.clone.back_ref) | copy-start | bytes 36868
  7.2 0.7 %copy-start.8 = (bf16[64,96]{1,0:T(8,128)(2,1)S(1)}, bf16[64,96]{1,0:T(8,128)(2,1)}, u32[]{:S(2)}) copy-start(bf16[64,96]{1,0:T(8,128)(2,1)} %constant.10.clone.into_ref) | copy-start | bytes 36868

commit v2 on v1

--- a/solution.py
+++ b/solution.py
@@ -153,6 +153,7 @@
 
 LANES = 128
 HALO = 136
+PARTS = 2
 MESH = pl.DeviceIdType.MESH
 
 
@@ -248,6 +249,18 @@
 def kernel(
     seq_size,
     ch_size,
+    proj_hbm,
+    short_hbm,
+    medium_hbm,
+    taps_hbm,
+    resid_hbm,
+    mix_hbm,
+    into_hbm,
+    back_hbm,
+    ahead_hbm,
+    behind_hbm,
+    turn_hbm,
+    out_ref,
     proj_ref,
     short_ref,
     medium_ref,
@@ -259,7 +272,8 @@
     ahead_ref,
     behind_ref,
     turn_ref,
-    out_ref,
+    stage_sem,
+    proj_sem,
     lines_t,
     feat_v,
     taps_out,
@@ -286,12 +300,43 @@
     me = lax.axis_index("seq")
     group = lax.axis_index("ch")
     chan, span = proj_ref.shape[1], proj_ref.shape[2]
-    short_span = short_ref.shape[0]
+    short_span = short_ref.shape[1]
     medium_span = medium_ref.shape[0]
-    each = chan // seq_size
+    each = chan // seq_size // PARTS
     blocks = span // LANES
     rows = seq_size * blocks
     slab = blocks * each
+    part_chan = chan // PARTS
+
+    proj_copies = {
+        stream: pltpu.make_async_copy(
+            proj_hbm.at[stream], proj_ref.at[stream], proj_sem.at[stream]
+        )
+        for stream in (2, 1, 0)
+    }
+    staged = {}
+    for i, (name, src, dst) in enumerate(
+        (
+            ("taps", taps_hbm, taps_ref),
+            ("short", short_hbm, short_ref),
+            ("medium", medium_hbm, medium_ref),
+            ("into", into_hbm, into_ref),
+            ("turn", turn_hbm, turn_ref),
+            ("ahead", ahead_hbm, ahead_ref),
+            ("behind", behind_hbm, behind_ref),
+            ("back", back_hbm, back_ref),
+            ("resid", resid_hbm, resid_ref),
+            ("mix", mix_hbm, mix_ref),
+        )
+    ):
+        staged[name] = pltpu.make_async_copy(src, dst, stage_sem.at[i])
+    proj_copies[2].start()
+    staged["taps"].start()
+    proj_copies[1].start()
+    proj_copies[0].start()
+    for name in staged:
+        if name != "taps":
+            staged[name].start()
 
     barrier = pltpu.get_barrier_semaphore()
     for step in range(1, seq_size):
@@ -310,15 +355,20 @@
             ].T
 
     def scatter_rows(dst, k, block):
-        for s in range(seq_size):
-            dst[s * slab + k * each : s * slab + (k + 1) * each, :] = block[
-                s * each : (s + 1) * each, :
-            ]
-
+        for part in range(PARTS):
+            for s in range(seq_size):
+                begin = s * slab + k * each
+                first = part * part_chan + s * each
+                dst[part, begin : begin + each, :] = block[first : first + each, :]
+
+    proj_copies[2].wait()
     transpose_in(2)
+    staged["taps"].wait()
     for k in range(blocks):
         scatter_rows(taps_out, k, taps_ref[:, k * LANES : (k + 1) * LANES])
+    proj_copies[1].wait()
     transpose_in(1)
+    proj_copies[0].wait()
     transpose_in(0)
     pl.semaphore_wait(barrier, seq_size - 1 + ch_size - 1)
 
@@ -348,7 +398,8 @@
         for copy in halo_copies():
             copy.start()
 
-    def exchange(src, dst, send, recv):
+    def exchange(src, dst, send, recv, part):
+        src, dst, send, recv = src.at[part], dst.at[part], send.at[part], recv.at[part]
         copies = []
         for step in range(1, seq_size):
             peer = lax.rem(me + step, seq_size)
@@ -368,7 +419,10 @@
         dst[own, :] = src[own, :]
         return copies
 
-    taps_copies = exchange(taps_out, taps_in, taps_send, taps_recv)
+    every = range(PARTS)
+    taps_copies = [exchange(taps_out, taps_in, taps_send, taps_recv, part) for part in every]
+    staged["short"].wait()
+    staged["medium"].wait()
 
     @pl.when(me == 0)
     def _():
@@ -384,7 +438,7 @@
         total = None
         for j in range(short_span):
             term = (
-                short_ref[j, stream : stream + 1, :]
+                short_ref[stream, j : j + 1, :]
                 * lines_t[stream, begin - j : begin - j + count, :]
             )
             total = term if total is None else total + term
@@ -411,44 +465,66 @@
         block = short(1, HALO + k * LANES, LANES) * smooth
         scatter_rows(carrier, k, block.T)
 
-    carrier_copies = exchange(carrier, carrier_in, carrier_send, carrier_recv)
-
-    for copy in taps_copies:
-        copy.wait_recv()
-    to_spectrum(taps_in, spec_filt, each, rows, into_ref, ahead_ref, turn_ref)
+    carrier_copies = [
+        exchange(carrier, carrier_in, carrier_send, carrier_recv, part) for part in every
+    ]
+
+    for name in ("into", "turn", "ahead", "behind", "back", "resid", "mix"):
+        staged[name].wait()
+    for part in every:
+        for copy in taps_copies[part]:
+            copy.wait_recv()
+        to_spectrum(
+            taps_in.at[part], spec_filt.at[part], each, rows, into_ref, ahead_ref, turn_ref
+        )
     for k in range(blocks):
         scatter_rows(gate, k, short(0, HALO + k * LANES, LANES).T)
     resid = jnp.broadcast_to(resid_ref[...], (LANES, chan)).T
 
-    for copy in carrier_copies:
-        copy.wait_recv()
-    to_spectrum(carrier_in, spec_val, each, rows, into_ref, ahead_ref, turn_ref)
-    from_spectrum(spec_val, spec_filt, answer, each, rows, back_ref, behind_ref, turn_ref)
-    answer_copies = exchange(answer, answer_in, answer_send, answer_recv)
-    for copy in answer_copies:
-        copy.wait_recv()
-
-    for s in range(seq_size):
-        weight = resid[s * each : (s + 1) * each, :]
-        for k in range(blocks):
-            part = slice(s * slab + k * each, s * slab + (k + 1) * each)
-            value = gate[part, :] * (answer_in[part, :] + weight * carrier[part, :])
-            gated[group, s * each : (s + 1) * each, k * LANES : (k + 1) * LANES] = value.astype(
-                jnp.bfloat16
+    answer_copies = []
+    for part in every:
+        for copy in carrier_copies[part]:
+            copy.wait_recv()
+        to_spectrum(carrier_in.at[part], spec_val, each, rows, into_ref, ahead_ref, turn_ref)
+        from_spectrum(
+            spec_val,
+            spec_filt.at[part],
+            answer.at[part],
+            each,
+            rows,
+            back_ref,
+            behind_ref,
+            turn_ref,
+        )
+        answer_copies.append(exchange(answer, answer_in, answer_send, answer_recv, part))
+
+    gated_copies = []
+    for part in every:
+        for copy in answer_copies[part]:
+            copy.wait_recv()
+        for s in range(seq_size):
+            first = part * part_chan + s * each
+            weight = resid[first : first + each, :]
+            for k in range(blocks):
+                piece = slice(s * slab + k * each, s * slab + (k + 1) * each)
+                value = gate[part, piece, :] * (
+                    answer_in[part, piece, :] + weight * carrier[part, piece, :]
+                )
+                gated[group, first : first + each, k * LANES : (k + 1) * LANES] = value.astype(
+                    jnp.bfloat16
+                )
+        lines = slice(part * part_chan, (part + 1) * part_chan)
+        for step in range(1, ch_size):
+            copy = pltpu.make_async_remote_copy(
+                src_ref=gated.at[group, lines, :],
+                dst_ref=gated.at[group, lines, :],
+                send_sem=gated_send.at[part, step],
+                recv_sem=gated_recv.at[part, step],
+                device_id={"ch": lax.rem(group + step, ch_size)},
+                device_id_type=MESH,
             )
-
-    gated_copies = []
-    for step in range(1, ch_size):
-        copy = pltpu.make_async_remote_copy(
-            src_ref=gated.at[group],
-            dst_ref=gated.at[group],
-            send_sem=gated_send.at[step],
-            recv_sem=gated_recv.at[step],
-            device_id={"ch": lax.rem(group + step, ch_size)},
-            device_id_type=MESH,
-        )
-        copy.start()
-        gated_copies.append(copy)
+            copy.start()
+            gated_copies.append((step, copy))
 
     def mixed(owner):
         weight = mix_ref[pl.ds(pl.multiple_of(owner * chan, LANES), chan), :]
@@ -458,7 +534,9 @@
 
     total = mixed(group)
     for step in range(1, ch_size):
-        gated_copies[step - 1].wait_recv()
+        for owner_step, copy in gated_copies:
+            if owner_step == step:
+                copy.wait_recv()
         total = total + mixed(lax.rem(group - step + ch_size, ch_size))
     out_ref[...] = total
 
@@ -467,7 +545,10 @@
         for copy in halo_copies():
             copy.wait_send()
 
-    for copy in taps_copies + carrier_copies + answer_copies + gated_copies:
+    for copies in taps_copies + carrier_copies + answer_copies:
+        for copy in copies:
+            copy.wait_send()
+    for _, copy in gated_copies:
         copy.wait_send()
 
 
@@ -480,15 +561,27 @@
     rows = seq_size * span // LANES
     tables = [jnp.asarray(table) for table in spectral_tables(rows)]
     vmem = pl.BlockSpec(memory_space=pltpu.VMEM)
-    plane = pltpu.VMEM((chan * span // LANES, LANES), jnp.float32)
-    spectrum = pltpu.VMEM((each * rows, 2 * LANES), jnp.float32)
+    plane = pltpu.VMEM((PARTS, chan * span // LANES // PARTS, LANES), jnp.float32)
+    spectrum = (each // PARTS * rows, 2 * LANES)
     dma = pltpu.SemaphoreType.DMA
+    operands = (
+        projected,
+        short_taps.transpose(1, 0, 2),
+        medium_taps,
+        global_kernel_taps,
+        residual_coefficient.reshape(1, chan),
+        mixer_weight,
+        *tables,
+    )
     return pl.pallas_call(
         functools.partial(kernel, seq_size, ch_size),
         out_shape=jax.ShapeDtypeStruct((mixer_weight.shape[1], span), jnp.float32),
-        in_specs=[vmem] * 11,
+        in_specs=[pl.BlockSpec(memory_space=pl.ANY)] * len(operands),
         out_specs=vmem,
-        scratch_shapes=[
+        scratch_shapes=[pltpu.VMEM(x.shape, x.dtype) for x in operands]
+        + [
+            dma((10,)),
+            dma((3,)),
             pltpu.VMEM((3, HALO + span, chan), jnp.float32),
             pltpu.VMEM((LANES + span, chan), jnp.float32),
             plane,
@@ -498,33 +591,25 @@
             plane,
             plane,
             plane,
-            spectrum,
-            spectrum,
+            pltpu.VMEM((PARTS, *spectrum), jnp.float32),
+            pltpu.VMEM(spectrum, jnp.float32),
             pltpu.VMEM((ch_size, chan, span), jnp.bfloat16),
             dma((2,)),
             dma((2,)),
-            dma((seq_size,)),
-            dma((seq_size,)),
-            dma((seq_size,)),
-            dma((seq_size,)),
-            dma((seq_size,)),
-            dma((seq_size,)),
-            dma((ch_size,)),
-            dma((ch_size,)),
+            dma((PARTS, seq_size)),
+            dma((PARTS, seq_size)),
+            dma((PARTS, seq_size)),
+            dma((PARTS, seq_size)),
+            dma((PARTS, seq_size)),
+            dma((PARTS, seq_size)),
+            dma((PARTS, ch_size)),
+            dma((PARTS, ch_size)),
         ],
         compiler_params=pltpu.CompilerParams(
-            collective_id=0, has_side_effects=True, vmem_limit_bytes=40 * 2**20
+            collective_id=0, has_side_effects=True, vmem_limit_bytes=60 * 2**20
         ),
         name="hyena",
-    )(
-        projected,
-        short_taps,
-        medium_taps,
-        global_kernel_taps,
-        residual_coefficient.reshape(1, chan),
-        mixer_weight,
-        *tables,
-    )
+    )(*operands)
 
 
 def block(

time: 43.3 us -> 36.9 us (0.85)
  local copies, waits for them, and re-layouts: 8.64 us -> 1.67 us
  Pallas kernels: 34.2 us -> 35 us
    unnamed x22 -> x1, local copies, waits for them, and re-layouts: 8.64 us -> 1.67 us
    pallas_call x1, Pallas kernels: 34.2 us -> 35 us  [fused(): pl.pallas_call(functools.partial(kernel, seq_size, ch_size), out_shape=ja...]
where the time goes in v2:
time: 36.9 us; the launch traced here: 36.7 us
  Pallas kernels  35 us (95%)
  local copies, waits for them, and re-layouts  1.67 us (5%)
    pallas_call x1, Pallas kernels, fused(): pl.pallas_call(functools.partial(kernel, seq_size, ch_size), out_shape=ja...  35 us
    unnamed x1, local copies, waits for them, and re-layouts  1.67 us

profile of v2, /device:TPU:0, one launch (start us, length us, event | category | flops | bytes accessed | tf_op | source)
XLA Modules:
  0.0 36.7 jit_solution(11089492718412482480)
XLA Ops:
  0.0 35.0 %hyena.1 = f32[128,512]{1,0:T(8,128)} custom-call(f32[3,128,512]{2,1,0:T(8,128)} %proj_hbm.1, f32[3,7,128]{2,1,0:T(8,128)} %bitcast.2, f32[128,128]{1,0:T(8,128)} %medium_hbm.1, f32[128,512]{1,0:T(8,128)} %taps_hbm.1, f32[1,128]{1,0:T(1,128)} %bitcast.3, bf16[512,128]{1,0:T(8,128)(2,1)} %mix_hbm.1, bf16[64,96]{1,0:T(8,128)(2,1)} %constant.10.clone.into_hbm, ...), custom_call_target="tpu_custom_call" | custom-call | tf_op jit(solution)/shard_map/hyena/pallas_call | solution.py:576
  35.0 1.7 %copy.13 = f32[128,512]{1,0:T(8,128)} copy(f32[128,512]{1,0:T(8,128)} %hyena.1) | data formatting | bytes 524288

commit v3 on v2

--- a/solution.py
+++ b/solution.py
@@ -286,6 +286,10 @@
     spec_filt,
     spec_val,
     gated,
+    gathered,
+    weights,
+    mixed_out,
+    mixed_in,
     halo_send,
     halo_recv,
     taps_send,
@@ -296,6 +300,10 @@
     answer_recv,
     gated_send,
     gated_recv,
+    weights_send,
+    weights_recv,
+    mixed_send,
+    mixed_recv,
 ):
     me = lax.axis_index("seq")
     group = lax.axis_index("ch")
@@ -307,6 +315,7 @@
     rows = seq_size * blocks
     slab = blocks * each
     part_chan = chan // PARTS
+    share = span // ch_size
 
     proj_copies = {
         stream: pltpu.make_async_copy(
@@ -423,6 +432,20 @@
     taps_copies = [exchange(taps_out, taps_in, taps_send, taps_recv, part) for part in every]
     staged["short"].wait()
     staged["medium"].wait()
+    staged["mix"].wait()
+    weight_copies = []
+    for step in range(1, ch_size):
+        copy = pltpu.make_async_remote_copy(
+            src_ref=mix_ref,
+            dst_ref=weights.at[group],
+            send_sem=weights_send.at[step],
+            recv_sem=weights_recv.at[step],
+            device_id={"ch": lax.rem(group + step, ch_size)},
+            device_id_type=MESH,
+        )
+        copy.start()
+        weight_copies.append(copy)
+    weights[group] = mix_ref[...]
 
     @pl.when(me == 0)
     def _():
@@ -469,7 +492,7 @@
         exchange(carrier, carrier_in, carrier_send, carrier_recv, part) for part in every
     ]
 
-    for name in ("into", "turn", "ahead", "behind", "back", "resid", "mix"):
+    for name in ("into", "turn", "ahead", "behind", "back", "resid"):
         staged[name].wait()
     for part in every:
         for copy in taps_copies[part]:
@@ -510,35 +533,62 @@
                 value = gate[part, piece, :] * (
                     answer_in[part, piece, :] + weight * carrier[part, piece, :]
                 )
-                gated[group, first : first + each, k * LANES : (k + 1) * LANES] = value.astype(
+                owner, column = divmod(k * LANES, share)
+                gated[owner, first : first + each, column : column + LANES] = value.astype(
                     jnp.bfloat16
                 )
         lines = slice(part * part_chan, (part + 1) * part_chan)
         for step in range(1, ch_size):
+            peer = lax.rem(group + step, ch_size)
             copy = pltpu.make_async_remote_copy(
-                src_ref=gated.at[group, lines, :],
-                dst_ref=gated.at[group, lines, :],
+                src_ref=gated.at[peer, lines, :],
+                dst_ref=gathered.at[group, lines, :],
                 send_sem=gated_send.at[part, step],
                 recv_sem=gated_recv.at[part, step],
-                device_id={"ch": lax.rem(group + step, ch_size)},
+                device_id={"ch": peer},
                 device_id_type=MESH,
             )
             copy.start()
-            gated_copies.append((step, copy))
+            gated_copies.append(copy)
+        gathered[group, lines, :] = gated[group, lines, :]
+
+    for copy in weight_copies + gated_copies:
+        copy.wait_recv()
+    signal = gathered[...].reshape(ch_size * chan, share)
 
     def mixed(owner):
-        weight = mix_ref[pl.ds(pl.multiple_of(owner * chan, LANES), chan), :]
         return lax.dot_general(
-            weight, gated[owner], (((0,), (0,)), ((), ())), preferred_element_type=jnp.float32
-        )
-
-    total = mixed(group)
+            weights[owner], signal, (((0,), (0,)), ((), ())), preferred_element_type=jnp.float32
+        )
+
+    mixed_copies = []
     for step in range(1, ch_size):
-        for owner_step, copy in gated_copies:
-            if owner_step == step:
-                copy.wait_recv()
-        total = total + mixed(lax.rem(group - step + ch_size, ch_size))
-    out_ref[...] = total
+        peer = lax.rem(group + step, ch_size)
+        mixed_out[step] = mixed(peer).astype(jnp.bfloat16)
+        copy = pltpu.make_async_remote_copy(
+            src_ref=mixed_out.at[step],
+            dst_ref=mixed_in.at[group],
+            send_sem=mixed_send.at[step],
+            recv_sem=mixed_recv.at[step],
+            device_id={"ch": peer},
+            device_id_type=MESH,
+        )
+        copy.start()
+        mixed_copies.append(copy)
+    own = mixed(group)
+    for copy in mixed_copies:
+        copy.wait_recv()
+    for owner in range(ch_size):
+        columns = slice(owner * share, (owner + 1) * share)
+
+        @pl.when(group == owner)
+        def _():
+            out_ref[:, columns] = own
+
+        @pl.when(group != owner)
+        def _():
+            out_ref[:, columns] = mixed_in[owner].astype(jnp.float32)
+
 
     @pl.when(me < seq_size - 1)
     def _():
@@ -548,7 +598,7 @@
     for copies in taps_copies + carrier_copies + answer_copies:
         for copy in copies:
             copy.wait_send()
-    for _, copy in gated_copies:
+    for copy in gated_copies + weight_copies + mixed_copies:
         copy.wait_send()
 
 
@@ -593,7 +643,11 @@
             plane,
             pltpu.VMEM((PARTS, *spectrum), jnp.float32),
             pltpu.VMEM(spectrum, jnp.float32),
-            pltpu.VMEM((ch_size, chan, span), jnp.bfloat16),
+            pltpu.VMEM((ch_size, chan, span // ch_size), jnp.bfloat16),
+            pltpu.VMEM((ch_size, chan, span // ch_size), jnp.bfloat16),
+            pltpu.VMEM((ch_size, *mixer_weight.shape), jnp.bfloat16),
+            pltpu.VMEM((ch_size, mixer_weight.shape[1], span // ch_size), jnp.bfloat16),
+            pltpu.VMEM((ch_size, mixer_weight.shape[1], span // ch_size), jnp.bfloat16),
             dma((2,)),
             dma((2,)),
             dma((PARTS, seq_size)),
@@ -604,6 +658,10 @@
             dma((PARTS, seq_size)),
             dma((PARTS, ch_size)),
             dma((PARTS, ch_size)),
+            dma((ch_size,)),
+            dma((ch_size,)),
+            dma((ch_size,)),
+            dma((ch_size,)),
         ],
         compiler_params=pltpu.CompilerParams(
             collective_id=0, has_side_effects=True, vmem_limit_bytes=60 * 2**20
@@ -627,7 +685,7 @@
     each = chan // lax.axis_size("seq")
     fits = (
         chan == LANES
-        and span % LANES == 0
+        and span % (LANES * lax.axis_size("ch")) == 0
         and span >= HALO
         and each % 16 == 0
         and medium_taps.shape[0] == LANES

time: 36.9 us -> 33.8 us (0.916)
  Pallas kernels: 35 us -> 32 us
    pallas_call x1, Pallas kernels: 35 us -> 32 us  [fused(): pl.pallas_call(functools.partial(kernel, seq_size, ch_size), out_shape=ja...]
where the time goes in v3:
time: 33.8 us; the launch traced here: 33.7 us
  Pallas kernels  32 us (95%)
  local copies, waits for them, and re-layouts  1.67 us (5%)
    pallas_call x1, Pallas kernels, fused(): pl.pallas_call(functools.partial(kernel, seq_size, ch_size), out_shape=ja...  32 us
    unnamed x1, local copies, waits for them, and re-layouts  1.67 us

profile of v3, /device:TPU:0, one launch (start us, length us, event | category | flops | bytes accessed | tf_op | source)
XLA Modules:
  0.0 33.7 jit_solution(15912116631497982443)
XLA Ops:
  0.0 32.0 %hyena.1 = f32[128,512]{1,0:T(8,128)} custom-call(f32[3,128,512]{2,1,0:T(8,128)} %proj_hbm.1, f32[3,7,128]{2,1,0:T(8,128)} %bitcast.2, f32[128,128]{1,0:T(8,128)} %medium_hbm.1, f32[128,512]{1,0:T(8,128)} %taps_hbm.1, f32[1,128]{1,0:T(1,128)} %bitcast.3, bf16[512,128]{1,0:T(8,128)(2,1)} %mix_hbm.1, bf16[64,96]{1,0:T(8,128)(2,1)} %constant.10.clone.into_hbm, ...), custom_call_target="tpu_custom_call" | custom-call | tf_op jit(solution)/shard_map/hyena/pallas_call | solution.py:626
  32.0 1.7 %copy.13 = f32[128,512]{1,0:T(8,128)} copy(f32[128,512]{1,0:T(8,128)} %hyena.1) | data formatting | bytes 524288

commit v4 on v3

--- a/solution.py
+++ b/solution.py
@@ -289,7 +289,6 @@
     gathered,
     weights,
     mixed_out,
-    mixed_in,
     halo_send,
     halo_recv,
     taps_send,
@@ -304,6 +303,7 @@
     weights_recv,
     mixed_send,
     mixed_recv,
+    own_sem,
 ):
     me = lax.axis_index("seq")
     group = lax.axis_index("ch")
@@ -372,13 +372,6 @@
 
     proj_copies[2].wait()
     transpose_in(2)
-    staged["taps"].wait()
-    for k in range(blocks):
-        scatter_rows(taps_out, k, taps_ref[:, k * LANES : (k + 1) * LANES])
-    proj_copies[1].wait()
-    transpose_in(1)
-    proj_copies[0].wait()
-    transpose_in(0)
     pl.semaphore_wait(barrier, seq_size - 1 + ch_size - 1)
 
     def halo_copies():
@@ -404,18 +397,18 @@
 
     @pl.when(me < seq_size - 1)
     def _():
-        for copy in halo_copies():
-            copy.start()
-
-    def exchange(src, dst, send, recv, part):
-        src, dst, send, recv = src.at[part], dst.at[part], send.at[part], recv.at[part]
+        halo_copies()[0].start()
+
+    def exchange(src, dst, send, recv, part, lane, begin, count):
+        src, dst = src.at[part], dst.at[part]
+        send, recv = send.at[lane], recv.at[lane]
         copies = []
         for step in range(1, seq_size):
             peer = lax.rem(me + step, seq_size)
             copies.append(
                 pltpu.make_async_remote_copy(
-                    src_ref=src.at[pl.ds(pl.multiple_of(peer * slab, 8), slab), :],
-                    dst_ref=dst.at[pl.ds(pl.multiple_of(me * slab, 8), slab), :],
+                    src_ref=src.at[pl.ds(pl.multiple_of(peer * slab + begin, 8), count), :],
+                    dst_ref=dst.at[pl.ds(pl.multiple_of(me * slab + begin, 8), count), :],
                     send_sem=send.at[step],
                     recv_sem=recv.at[step],
                     device_id={"seq": peer},
@@ -424,12 +417,26 @@
             )
         for copy in copies:
             copy.start()
-        own = pl.ds(pl.multiple_of(me * slab, 8), slab)
+        own = pl.ds(pl.multiple_of(me * slab + begin, 8), count)
         dst[own, :] = src[own, :]
         return copies
 
     every = range(PARTS)
-    taps_copies = [exchange(taps_out, taps_in, taps_send, taps_recv, part) for part in every]
+    proj_copies[1].wait()
+    transpose_in(1)
+    proj_copies[0].wait()
+    transpose_in(0)
+
+    @pl.when(me < seq_size - 1)
+    def _():
+        halo_copies()[1].start()
+
+    staged["taps"].wait()
+    for k in range(blocks):
+        scatter_rows(taps_out, k, taps_ref[:, k * LANES : (k + 1) * LANES])
+    taps_copies = [
+        exchange(taps_out, taps_in, taps_send, taps_recv, part, part, 0, slab) for part in every
+    ]
     staged["short"].wait()
     staged["medium"].wait()
     staged["mix"].wait()
@@ -447,16 +454,6 @@
         weight_copies.append(copy)
     weights[group] = mix_ref[...]
 
-    @pl.when(me == 0)
-    def _():
-        lines_t[2, 0:HALO, :] = jnp.zeros((HALO, chan), jnp.float32)
-        lines_t[0:2, HALO - 8 : HALO, :] = jnp.zeros((2, 8, chan), jnp.float32)
-
-    @pl.when(me > 0)
-    def _():
-        for copy in halo_copies():
-            copy.wait_recv()
-
     def short(stream, begin, count):
         total = None
         for j in range(short_span):
@@ -467,12 +464,15 @@
             total = term if total is None else total + term
         return total
 
-    for begin in range(0, LANES + span, LANES):
+    def featured(begin):
         feat_v[begin : begin + LANES, :] = short(2, HALO - LANES + begin, LANES)
 
+    for begin in range(2 * LANES, LANES + span, LANES):
+        featured(begin)
+
     tile = 8
 
-    for k in range(blocks):
+    def carry(k):
         base = (k + 1) * LANES
 
         def taps_body(m, total):
@@ -488,9 +488,41 @@
         block = short(1, HALO + k * LANES, LANES) * smooth
         scatter_rows(carrier, k, block.T)
 
-    carrier_copies = [
-        exchange(carrier, carrier_in, carrier_send, carrier_recv, part) for part in every
-    ]
+    def send_carrier(wave, begin, count):
+        return [
+            exchange(
+                carrier,
+                carrier_in,
+                carrier_send,
+                carrier_recv,
+                part,
+                part * 2 + wave,
+                begin,
+                count,
+            )
+            for part in every
+        ]
+
+    for k in range(blocks - 1, 1, -1):
+        carry(k)
+    early = send_carrier(0, 2 * each, slab - 2 * each)
+
+    @pl.when(me == 0)
+    def _():
+        lines_t[2, 0:HALO, :] = jnp.zeros((HALO, chan), jnp.float32)
+        lines_t[0:2, HALO - 8 : HALO, :] = jnp.zeros((2, 8, chan), jnp.float32)
+
+    @pl.when(me > 0)
+    def _():
+        for copy in halo_copies():
+            copy.wait_recv()
+
+    featured(LANES)
+    featured(0)
+    carry(1)
+    carry(0)
+    late = send_carrier(1, 0, 2 * each)
+    carrier_copies = [early[part] + late[part] for part in every]
 
     for name in ("into", "turn", "ahead", "behind", "back", "resid"):
         staged[name].wait()
@@ -519,7 +551,7 @@
             behind_ref,
             turn_ref,
         )
-        answer_copies.append(exchange(answer, answer_in, answer_send, answer_recv, part))
+        answer_copies.append(exchange(answer, answer_in, answer_send, answer_recv, part, part, 0, slab))
 
     gated_copies = []
     for part in every:
@@ -561,13 +593,14 @@
             weights[owner], signal, (((0,), (0,)), ((), ())), preferred_element_type=jnp.float32
         )
 
+    mine = pl.ds(pl.multiple_of(group * share, LANES), share)
     mixed_copies = []
     for step in range(1, ch_size):
         peer = lax.rem(group + step, ch_size)
         mixed_out[step] = mixed(peer).astype(jnp.bfloat16)
         copy = pltpu.make_async_remote_copy(
             src_ref=mixed_out.at[step],
-            dst_ref=mixed_in.at[group],
+            dst_ref=out_ref.at[:, mine],
             send_sem=mixed_send.at[step],
             recv_sem=mixed_recv.at[step],
             device_id={"ch": peer},
@@ -575,20 +608,12 @@
         )
         copy.start()
         mixed_copies.append(copy)
-    own = mixed(group)
+    mixed_out[0] = mixed(group).astype(jnp.bfloat16)
+    own = pltpu.make_async_copy(mixed_out.at[0], out_ref.at[:, mine], own_sem)
+    own.start()
     for copy in mixed_copies:
         copy.wait_recv()
-    for owner in range(ch_size):
-        columns = slice(owner * share, (owner + 1) * share)
-
-        @pl.when(group == owner)
-        def _():
-            out_ref[:, columns] = own
-
-        @pl.when(group != owner)
-        def _():
-            out_ref[:, columns] = mixed_in[owner].astype(jnp.float32)
-
+    own.wait()
 
     @pl.when(me < seq_size - 1)
     def _():
@@ -610,7 +635,6 @@
     each = chan // seq_size
     rows = seq_size * span // LANES
     tables = [jnp.asarray(table) for table in spectral_tables(rows)]
-    vmem = pl.BlockSpec(memory_space=pltpu.VMEM)
     plane = pltpu.VMEM((PARTS, chan * span // LANES // PARTS, LANES), jnp.float32)
     spectrum = (each // PARTS * rows, 2 * LANES)
     dma = pltpu.SemaphoreType.DMA
@@ -623,11 +647,11 @@
         mixer_weight,
         *tables,
     )
-    return pl.pallas_call(
+    mixed = pl.pallas_call(
         functools.partial(kernel, seq_size, ch_size),
-        out_shape=jax.ShapeDtypeStruct((mixer_weight.shape[1], span), jnp.float32),
+        out_shape=jax.ShapeDtypeStruct((mixer_weight.shape[1], span), jnp.bfloat16),
         in_specs=[pl.BlockSpec(memory_space=pl.ANY)] * len(operands),
-        out_specs=vmem,
+        out_specs=pl.BlockSpec(memory_space=pl.ANY),
         scratch_shapes=[pltpu.VMEM(x.shape, x.dtype) for x in operands]
         + [
             dma((10,)),
@@ -647,13 +671,12 @@
             pltpu.VMEM((ch_size, chan, span // ch_size), jnp.bfloat16),
             pltpu.VMEM((ch_size, *mixer_weight.shape), jnp.bfloat16),
             pltpu.VMEM((ch_size, mixer_weight.shape[1], span // ch_size), jnp.bfloat16),
-            pltpu.VMEM((ch_size, mixer_weight.shape[1], span // ch_size), jnp.bfloat16),
             dma((2,)),
             dma((2,)),
             dma((PARTS, seq_size)),
             dma((PARTS, seq_size)),
-            dma((PARTS, seq_size)),
-            dma((PARTS, seq_size)),
+            dma((PARTS * 2, seq_size)),
+            dma((PARTS * 2, seq_size)),
             dma((PARTS, seq_size)),
             dma((PARTS, seq_size)),
             dma((PARTS, ch_size)),
@@ -662,12 +685,14 @@
             dma((ch_size,)),
             dma((ch_size,)),
             dma((ch_size,)),
+            dma(()),
         ],
         compiler_params=pltpu.CompilerParams(
             collective_id=0, has_side_effects=True, vmem_limit_bytes=60 * 2**20
         ),
         name="hyena",
     )(*operands)
+    return mixed.astype(jnp.float32)
 
 
 def block(

time: 33.8 us -> 31.2 us (0.923)
  Pallas kernels: 32 us -> 29.4 us
  local copies, waits for them, and re-layouts: 1.67 us -> 0 us
  other arithmetic: 0 us -> 1.63 us
    pallas_call x1, Pallas kernels: 32 us -> 29.4 us  [fused(): pl.pallas_call(functools.partial(kernel, seq_size, ch_size), out_shape=ja...]
    unnamed x1 -> x0, local copies, waits for them, and re-layouts: 1.67 us -> none
    convert_element_type x0 -> x1, other arithmetic: none -> 1.63 us  [fused(): return mixed.astype(jnp.float32)]
where the time goes in v4:
time: 31.2 us; the launch traced here: 31 us
  Pallas kernels  29.4 us (94%)
  other arithmetic  1.63 us (5%)
    pallas_call x1, Pallas kernels, fused(): pl.pallas_call(functools.partial(kernel, seq_size, ch_size), out_shape=ja...  29.4 us
    convert_element_type x1, other arithmetic, fused(): return mixed.astype(jnp.float32)  1.63 us

profile of v4, /device:TPU:0, one launch (start us, length us, event | category | flops | bytes accessed | tf_op | source)
XLA Modules:
  0.0 31.0 jit_solution(2045110323217726794)
XLA Ops:
  0.0 29.4 %hyena.1 = bf16[128,512]{1,0:T(8,128)(2,1)} custom-call(f32[3,128,512]{2,1,0:T(8,128)} %proj_hbm.1, f32[3,7,128]{2,1,0:T(8,128)} %bitcast.2, f32[128,128]{1,0:T(8,128)} %medium_hbm.1, f32[128,512]{1,0:T(8,128)} %taps_hbm.1, f32[1,128]{1,0:T(1,128)} %bitcast.3, bf16[512,128]{1,0:T(8,128)(2,1)} %mix_hbm.1, bf16[64,96]{1,0:T(8,128)(2,1)} %constant.10.clone.into_hbm, ...), custom_call_target="tpu_custom_call" | custom-call | tf_op jit(solution)/shard_map/hyena/pallas_call | solution.py:650
  29.4 1.6 %convert_element_type.3 = f32[128,512]{1,0:T(8,128)} convert(bf16[128,512]{1,0:T(8,128)(2,1)} %hyena.1) | non-fusion elementwise | flops 65536 | bytes 393216 | tf_op jit(solution)/shard_map/convert_element_type | solution.py:695

commit v5 on v4

--- a/solution.py
+++ b/solution.py
@@ -288,6 +288,7 @@
     gated,
     gathered,
     weights,
+    turned_weights,
     mixed_out,
     halo_send,
     halo_recv,
@@ -552,6 +553,11 @@
             turn_ref,
         )
         answer_copies.append(exchange(answer, answer_in, answer_send, answer_recv, part, part, 0, slab))
+
+    for copy in weight_copies:
+        copy.wait_recv()
+    for owner in range(ch_size):
+        turned_weights[owner] = weights[owner].astype(jnp.float32).T.astype(jnp.bfloat16)
 
     gated_copies = []
     for part in every:
@@ -584,14 +590,12 @@
             gated_copies.append(copy)
         gathered[group, lines, :] = gated[group, lines, :]
 
-    for copy in weight_copies + gated_copies:
+    for copy in gated_copies:
         copy.wait_recv()
     signal = gathered[...].reshape(ch_size * chan, share)
 
     def mixed(owner):
-        return lax.dot_general(
-            weights[owner], signal, (((0,), (0,)), ((), ())), preferred_element_type=jnp.float32
-        )
+        return dot(turned_weights[owner], signal)
 
     mine = pl.ds(pl.multiple_of(group * share, LANES), share)
     mixed_copies = []
@@ -670,6 +674,7 @@
             pltpu.VMEM((ch_size, chan, span // ch_size), jnp.bfloat16),
             pltpu.VMEM((ch_size, chan, span // ch_size), jnp.bfloat16),
             pltpu.VMEM((ch_size, *mixer_weight.shape), jnp.bfloat16),
+            pltpu.VMEM((ch_size, *mixer_weight.shape[::-1]), jnp.bfloat16),
             pltpu.VMEM((ch_size, mixer_weight.shape[1], span // ch_size), jnp.bfloat16),
             dma((2,)),
             dma((2,)),

time: 31.2 us -> 31.4 us (level)
  no operation moved by 1% of the time
where the time goes in v5:
time: 31.4 us; the launch traced here: 31.2 us
  Pallas kernels  29.6 us (94%)
  other arithmetic  1.63 us (5%)
    pallas_call x1, Pallas kernels, fused(): pl.pallas_call(functools.partial(kernel, seq_size, ch_size), out_shape=ja...  29.6 us
    convert_element_type x1, other arithmetic, fused(): return mixed.astype(jnp.float32)  1.63 us

profile of v5, /device:TPU:0, one launch (start us, length us, event | category | flops | bytes accessed | tf_op | source)
XLA Modules:
  0.0 31.2 jit_solution(14766901931194364467)
XLA Ops:
  0.0 29.6 %hyena.1 = bf16[128,512]{1,0:T(8,128)(2,1)} custom-call(f32[3,128,512]{2,1,0:T(8,128)} %proj_hbm.1, f32[3,7,128]{2,1,0:T(8,128)} %bitcast.2, f32[128,128]{1,0:T(8,128)} %medium_hbm.1, f32[128,512]{1,0:T(8,128)} %taps_hbm.1, f32[1,128]{1,0:T(1,128)} %bitcast.3, bf16[512,128]{1,0:T(8,128)(2,1)} %mix_hbm.1, bf16[64,96]{1,0:T(8,128)(2,1)} %constant.10.clone.into_hbm, ...), custom_call_target="tpu_custom_call" | custom-call | tf_op jit(solution)/shard_map/hyena/pallas_call | solution.py:654
  29.6 1.6 %convert_element_type.3 = f32[128,512]{1,0:T(8,128)} convert(bf16[128,512]{1,0:T(8,128)(2,1)} %hyena.1) | non-fusion elementwise | flops 65536 | bytes 393216 | tf_op jit(solution)/shard_map/convert_element_type | solution.py:700
